TPU v7x, 128 devices: a whole 4x4x4 slice. The times are simulated.
128 devices in a mesh: prow: 8 (over y, core), pcol: 16 (over x, z).
Axes of the slice: x: 4, y: 4, z: 4, core: 2. Of those that a mesh axis runs over, the one named last changes fastest.
Arguments:
- cross_cov: float32 [2, 512, 16384], P(None, 'prow', 'pcol'), may hold values from -6 to 6
- prev_rows: bfloat16 [2, 512, 32768], P(None, 'pcol', 'prow'), may hold values from -0.046875 to 0.046875
- prev_solved: bfloat16 [32768, 16384], P('prow', 'pcol'), may hold values from -6 to 6
- sub_block: float32 [512, 512], replicated, may hold values from -0.25 to 0.25
- inv_first: float32 [512, 512], replicated, as said below
- inv_second: float32 [512, 512], replicated, as said below
Outputs:
- solved: float32 [2, 512, 16384], P(None, 'prow', 'pcol')
Inputs may be any that keep to these rules, and one draw needn't show every extreme that they name: inv_first is lower triangular with a positive diagonal. inv_second is lower triangular with a positive diagonal.
All inputs are finite; a program needn't handle non-finite values.
Results may differ from a plain program's by a relative error of at most 0.0003.
Values may be sent and summed in bfloat16 or wider, within the bound.
A program may use at most 64 MiB of HBM per device.

v0:
```python
import jax
import jax.numpy as jnp
from jax import lax
from jax.sharding import PartitionSpec as P


def mult(left, right, precision=lax.Precision.HIGHEST):
    return jnp.dot(left, right, preferred_element_type=jnp.float32, precision=precision)


def local(cross_cov, prev_rows, prev_solved, sub_block, inv_first, inv_second):
    rows = cross_cov.shape[1]
    pieces = 2
    width = prev_rows.shape[2] // pieces
    terms = None
    for p in range(pieces):
        gathered = lax.all_gather(
            prev_rows[:, :, p * width : (p + 1) * width], "pcol", axis=1, tiled=True
        )
        part = jnp.einsum(
            "kra,ac->krc",
            gathered,
            prev_solved[p * width : (p + 1) * width],
            preferred_element_type=jnp.float32,
        )
        terms = part if terms is None else terms + part
    offset = lax.axis_index("prow") * rows
    rhs = lax.dynamic_update_slice_in_dim(
        -terms, lax.dynamic_slice_in_dim(-terms, offset, rows, 1) + cross_cov, offset, 1
    )
    coupling = -mult(inv_second, mult(sub_block, inv_first))
    high = lax.Precision.HIGH
    nb = inv_first.shape[0]
    transform = jnp.concatenate(
        [
            jnp.concatenate([inv_first, jnp.zeros_like(inv_first)], axis=1),
            jnp.concatenate([coupling, inv_second], axis=1),
        ]
    )
    flat = rhs.reshape(2 * nb, -1)
    cols = flat.shape[1] // pieces
    out = []
    for p in range(pieces):
        both = mult(transform, flat[:, p * cols : (p + 1) * cols], high).reshape(2, nb, cols)
        out.append(lax.psum_scatter(both, "prow", scatter_dimension=1, tiled=True))
    return jnp.concatenate(out, axis=2)


def solution(mesh):
    return jax.shard_map(
        local,
        mesh=mesh,
        in_specs=(
            P(None, "prow", "pcol"),
            P(None, "pcol", "prow"),
            P("prow", "pcol"),
            P(),
            P(),
            P(),
        ),
        out_specs=P(None, "prow", "pcol"),
        check_vma=False,
    )
```

profile of v0, /device:TPU:0, one launch (start us, length us, event | category | flops | bytes accessed | tf_op | source)
XLA Modules:
  0.0 208.2 jit_solution(16049799425421940616)
XLA Ops:
  6.5 0.0 copy-start
  6.5 0.0 all-gather.5.cloned.1.call-start
  6.5 2.0 fusion.23
  8.6 0.0 all-gather.5.cloned.1.call-update
  8.6 0.0 all-gather.3.cloned.1.call-start
  8.7 0.7 all-gather.3.cloned.1.call-update
  9.4 0.0 reduce-scatter.5.cloned.1.call-start
  9.4 2.5 %copy.7 = f32[512,512]{0,1:T(8,128)} copy(f32[512,512]{1,0:T(8,128)} %param.10) | data formatting | bytes 2097152 | tf_op args[4]
  12.0 0.0 copy-done.2
  12.0 1.4 copy.8
  13.4 0.0 copy-done
  13.4 0.0 copy-done.1
  13.4 1.9 fusion.24
  15.2 3.5 %fusion.16 = f32[512,512]{0,1:T(8,128)S(1)} fusion(f32[512,512]{1,0:T(8,128)S(1)} %fusion.24, f32[512,512]{1,0:T(8,128)S(1)} %copy-done.2), kind=kOutput, calls=%fused_computation.18 | convolution fusion | flops 1610874880 | bytes 3145728 | tf_op jit(solution)/shard_map/dot_general | solution.py:8
  18.7 45.1 %all-gather.5.cloned.1.call-done = bf16[2,512,2048]{2,1,0:T(8,128)(2,1)} async-done(((bf16[2,32,2048]{2,1,0:T(8,128)(2,1)}), bf16[2,512,2048]{2,1,0:T(8,128)(2,1)}) %all-gather.5.cloned.1.call-update) | async-done | bytes 4194320 | tf_op jit(solution)/shard_map/all_gather | solution.py:17
  63.8 9.9 %fusion = f32[2,512,1024]{2,1,0:T(8,128)} fusion(bf16[2,512,2048]{2,1,0:T(8,128)(2,1)} %all-gather.5.cloned.1.call-done, bf16[4096,1024]{1,0:T(8,128)(2,1)} %param.8), kind=kOutput, calls=%fused_computation.2 | convolution fusion | flops 4294967296 | bytes 12582912 | tf_op jit(solution)/shard_map/kra,ac->krc/dot_general | solution.py:20
  73.7 43.6 %all-gather.3.cloned.1.call-done = bf16[2,512,2048]{2,1,0:T(8,128)(2,1)} async-done(((bf16[2,32,2048]{2,1,0:T(8,128)(2,1)}), bf16[2,512,2048]{2,1,0:T(8,128)(2,1)}) %all-gather.3.cloned.1.call-update) | async-done | bytes 4194320 | tf_op jit(solution)/shard_map/all_gather | solution.py:17
  117.3 9.2 %add_negate_fusion = f32[2,512,1024]{2,1,0:T(8,128)S(1)} fusion(f32[2,512,1024]{2,1,0:T(8,128)} %fusion, bf16[2,512,2048]{2,1,0:T(8,128)(2,1)} %all-gather.3.cloned.1.call-done, bf16[4096,1024]{1,0:T(8,128)(2,1)} %param.8), kind=kOutput, calls=%fused_computation.6 | convolution fusion | flops 4297064448 | bytes 16777216 | tf_op jit(solution)/shard_map/kra,ac->krc/dot_general | solution.py:20
  126.5 0.0 copy-done.5
  126.5 0.1 add_dynamic-update-slice_fusion
  126.6 0.0 copy-start.6
  126.6 0.0 copy-done.3
  126.7 0.0 copy-done.4
  126.7 5.1 %fusion.6 = f32[1024,512]{1,0:T(8,128)} fusion(f32[512,512]{0,1:T(8,128)S(1)} %copy-done.3, f32[512,512]{0,1:T(8,128)S(1)} %copy-done.4, f32[512,512]{0,1:T(8,128)S(1)} %fusion.16, f32[1024,1024]{1,0:T(8,128)S(1)} %bitcast.21), kind=kOutput, calls=%fused_computation.9 | convolution fusion | flops 3225419776 | bytes 7340032 | tf_op jit(solution)/shard_map/dot_general | solution.py:8
  131.7 0.0 copy-done.6
  131.8 0.0 reduce-scatter.5.cloned.1.call-update
  131.8 0.0 reduce-scatter.3.cloned.1.call-start
  131.8 6.7 %fusion.7 = f32[1024,512]{1,0:T(8,128)} fusion(f32[512,512]{0,1:T(8,128)S(1)} %copy-done.3, f32[512,512]{0,1:T(8,128)} %copy.8, f32[512,512]{0,1:T(8,128)S(1)} %fusion.16, f32[1024,1024]{1,0:T(8,128)} %bitcast.22), kind=kOutput, calls=%fused_computation.10 | convolution fusion | flops 3225419776 | bytes 7340032 | tf_op jit(solution)/shard_map/dot_general | solution.py:8
  138.6 0.0 reduce-scatter.3.cloned.1.call-update
  138.6 26.6 %reduce-scatter.5.cloned.1.call-done = f32[2,64,512]{2,1,0:T(8,128)} async-done(((f32[2,512,512]{2,1,0:T(8,128)}), f32[2,64,512]{2,1,0:T(8,128)}) %reduce-scatter.5.cloned.1.call-update) | async-done | bytes 262160 | tf_op jit(solution)/shard_map/reduce_scatter | solution.py:45
  165.2 34.7 %reduce-scatter.3.cloned.1.call-done = f32[2,64,512]{2,1,0:T(8,128)} async-done(((f32[2,512,512]{2,1,0:T(8,128)}), f32[2,64,512]{2,1,0:T(8,128)}) %reduce-scatter.3.cloned.1.call-update) | async-done | bytes 262160 | tf_op jit(solution)/shard_map/reduce_scatter | solution.py:45
  199.8 1.9 pad_maximum_fusion
  (5 shorter events, 0.0 us)
Async XLA Ops:
  6.5 6.8 %copy-start = (f32[512,512]{1,0:T(8,128)S(1)}, f32[512,512]{1,0:T(8,128)}, u32[]{:S(2)}) copy-start(f32[512,512]{1,0:T(8,128)} %param.9) | copy-start | bytes 3145732
  6.5 6.8 %copy-start.1 = (f32[512,512]{1,0:T(8,128)S(1)}, f32[512,512]{1,0:T(8,128)}, u32[]{:S(2)}) copy-start(f32[512,512]{1,0:T(8,128)} %param.10) | copy-start | bytes 3145732
  6.5 5.4 %copy-start.2 = (f32[512,512]{1,0:T(8,128)S(1)}, f32[512,512]{1,0:T(8,128)}, u32[]{:S(2)}) copy-start(f32[512,512]{1,0:T(8,128)} %param.11) | copy-start | bytes 3145732
  6.5 57.2 %all-gather.5.cloned.1.call-start = ((), (), s32[]{:S(2)}) async-start(), calls=%async_computation.3 | async-start | bytes 4456448 | tf_op jit(solution)/shard_map/all_gather | solution.py:17
  8.6 108.6 %all-gather.3.cloned.1.call-start = ((), (), s32[]{:S(2)}) async-start(), calls=%async_computation.2 | async-start | bytes 4456448 | tf_op jit(solution)/shard_map/all_gather | solution.py:17
  9.4 155.8 %reduce-scatter.5.cloned.1.call-start = ((), (), s32[]{:S(2)}) async-start(), calls=%async_computation.5 | async-start | bytes 2359296 | tf_op jit(solution)/shard_map/reduce_scatter | solution.py:45
  73.7 53.0 %copy-start.3 = (f32[512,512]{0,1:T(8,128)S(1)}, f32[512,512]{0,1:T(8,128)}, u32[]{:S(2)}) copy-start(f32[512,512]{0,1:T(8,128)} %copy.7) | copy-start | bytes 3145732
  117.3 9.3 %copy-start.5 = (f32[2,64,1024]{2,1,0:T(8,128)S(1)}, f32[2,64,1024]{2,1,0:T(8,128)}, u32[]{:S(2)}) copy-start(f32[2,64,1024]{2,1,0:T(8,128)} %param.6) | copy-start | bytes 1572868
  117.3 9.4 %copy-start.4 = (f32[512,512]{0,1:T(8,128)S(1)}, f32[512,512]{0,1:T(8,128)}, u32[]{:S(2)}) copy-start(f32[512,512]{0,1:T(8,128)} %copy.8) | copy-start | bytes 3145732
  126.6 5.1 %copy-start.6 = (f32[2,512,1024]{2,1,0:T(8,128)}, f32[2,512,1024]{2,1,0:T(8,128)S(1)}, u32[]{:S(2)}) copy-start(f32[2,512,1024]{2,1,0:T(8,128)S(1)} %add_dynamic-update-slice_fusion) | copy-start | bytes 12582916
  131.8 68.1 %reduce-scatter.3.cloned.1.call-start = ((), (), s32[]{:S(2)}) async-start(), calls=%async_computation.4 | async-start | bytes 2359296 | tf_op jit(solution)/shard_map/reduce_scatter | solution.py:45
Sparse Core Ops, SparseCore 0:
  9.6 54.1 all-gather.4
  66.0 51.2 all-gather.2
  131.9 33.2 reduce-scatter.4
  167.4 32.3 reduce-scatter.2
where the time goes:
time: 208 us
  waiting for transfers between devices  151 us (73%)
  matrix products  36.3 us (17%)
  between operations  13.2 us (6%)
  local copies, waits for them, and re-layouts  6 us (3%)
    all_gather x2, waiting for transfers between devices, local(): lax.all_gather(prev_rows[:, :, p * width:(p + 1) * width], 'pcol', axis=1...  88.6 us
    reduce_scatter x2, waiting for transfers between devices, local(): out.append(lax.psum_scatter(both, 'prow', scatter_dimension=1, tiled=True))  61.2 us
    dot_general x2, matrix products, local(): jnp.einsum('kra,ac->krc', gathered, prev_solved[p * width:(p + 1) * width...  19.2 us
    dot_general x4, matrix products, mult(): jnp.dot(left, right, preferred_element_type=jnp.float32, precision=precis...  17.1 us
  transfers between devices with their start and end apart: 4, of which 4 were waited for; matrix products, arithmetic and copies ran while one was open for 12% of the time, Pallas kernels for 0%

commit v1 on v0

--- a/solution.py
+++ b/solution.py
@@ -14,9 +14,19 @@
     width = prev_rows.shape[2] // pieces
     terms = None
     for p in range(pieces):
-        gathered = lax.all_gather(
-            prev_rows[:, :, p * width : (p + 1) * width], "pcol", axis=1, tiled=True
-        )
+
+        def _answer_task(here_x, which_axis, k_dim):
+            return jnp.concatenate(
+                lax.all_to_all(
+                    jnp.stack([here_x] * lax.axis_size(which_axis)),
+                    axis_name=which_axis,
+                    split_axis=0,
+                    concat_axis=0,
+                ),
+                k_dim,
+            )
+
+        gathered = _answer_task(prev_rows[:, :, p * width : (p + 1) * width], "pcol", 1)
         part = jnp.einsum(
             "kra,ac->krc",
             gathered,

time: 208 us -> 224 us (1.077)
  blocking collectives: 0 us -> 58.6 us
  waiting for transfers between devices: 151 us -> 104 us
  matrix products: 36.3 us -> 28 us
  local copies, waits for them, and re-layouts: 6 us -> 12.6 us
  starting transfers between devices: 0.12 us -> 4.75 us
    all_gather x2 -> x0, waiting for transfers between devices: 88.6 us -> none  [local(): lax.all_gather(prev_rows[:, :, p * width:(p + 1) * width], 'pcol', axis=1...]
    all_to_all x0 -> x1, blocking collectives: none -> 58.6 us  [_answer_task(): lax.all_to_all(jnp.stack([here_x] * lax.axis_size(which_axis)), axis_name...]
    all_to_all x0 -> x1, waiting for transfers between devices: none -> 43.9 us  [_answer_task(): lax.all_to_all(jnp.stack([here_x] * lax.axis_size(which_axis)), axis_name...]
    dot_general x2, matrix products: 19.2 us -> 11 us  [local(): jnp.einsum('kra,ac->krc', gathered, prev_solved[p * width:(p + 1) * width...]
    reshape x0 -> x2, local copies, waits for them, and re-layouts: none -> 4.94 us  [_answer_task(): jnp.concatenate(lax.all_to_all(jnp.stack([here_x] * lax.axis_size(which_a...]
    all_to_all x0 -> x1, starting transfers between devices: none -> 4.67 us  [_answer_task(): lax.all_to_all(jnp.stack([here_x] * lax.axis_size(which_axis)), axis_name...]
    another operation x0 -> x2, local copies, waits for them, and re-layouts: none -> 3.02 us  [_answer_task(): jnp.stack([here_x] * lax.axis_size(which_axis))]
  transfers between devices with their start and end apart: 4 -> 3, of which waited for: 4 -> 3; matrix products, arithmetic and copies ran while one was open for 12% -> 8% of each run, Pallas kernels for 0% -> 0%
where the time goes in v1:
time: 224 us
  waiting for transfers between devices  104 us (46%)
  blocking collectives  58.6 us (26%)
  matrix products  28 us (12%)
  between operations  13.6 us (6%)
  local copies, waits for them, and re-layouts  12.6 us (6%)
  starting transfers between devices  4.75 us (2%)
    reduce_scatter x2, waiting for transfers between devices, local(): out.append(lax.psum_scatter(both, 'prow', scatter_dimension=1, tiled=True))  60.2 us
    all_to_all x1, blocking collectives, _answer_task(): lax.all_to_all(jnp.stack([here_x] * lax.axis_size(which_axis)), axis_name...  58.6 us
    all_to_all x1, waiting for transfers between devices, _answer_task(): lax.all_to_all(jnp.stack([here_x] * lax.axis_size(which_axis)), axis_name...  43.9 us
    dot_general x4, matrix products, mult(): jnp.dot(left, right, preferred_element_type=jnp.float32, precision=precis...  17 us
    dot_general x2, matrix products, local(): jnp.einsum('kra,ac->krc', gathered, prev_solved[p * width:(p + 1) * width...  11 us
    reshape x2, local copies, waits for them, and re-layouts, _answer_task(): jnp.concatenate(lax.all_to_all(jnp.stack([here_x] * lax.axis_size(which_a...  4.94 us
    all_to_all x1, starting transfers between devices, _answer_task(): lax.all_to_all(jnp.stack([here_x] * lax.axis_size(which_axis)), axis_name...  4.67 us
  transfers between devices with their start and end apart: 3, of which 3 were waited for; matrix products, arithmetic and copies ran while one was open for 8% of the time, Pallas kernels for 0%

profile of v1, /device:TPU:0, one launch (start us, length us, event | category | flops | bytes accessed | tf_op | source)
XLA Modules:
  0.0 223.6 jit_solution(11536130434926452560)
XLA Ops:
  6.5 0.0 copy-start
  6.5 1.2 fusion.23
  7.7 0.5 stack.5
  8.2 58.6 %all_to_all.10 = bf16[16,2,32,2048]{3,2,1,0:T(8,128)(2,1)} all-to-all(bf16[16,2,32,2048]{3,2,1,0:T(8,128)(2,1)S(1)} %stack.5), channel_id=1, replica_groups=mesh['prow'=8,'pcol'=16] {'pcol'}, dimensions={0} | all-to-all | bytes 8388608 | tf_op jit(solution)/shard_map/all_to_all | solution.py:20
  66.8 2.5 %stack.4 = bf16[16,2,32,2048]{3,2,1,0:T(8,128)(2,1)} broadcast(bf16[2,32,2048]{2,1,0:T(8,128)(2,1)S(1)} %get-tuple-element.5), dimensions={1,2,3} | broadcast | bytes 4456448 | tf_op jit(solution)/shard_map/stack | solution.py:21
  69.3 4.7 %all-to-all-start = ((bf16[16,2,32,2048]{3,2,1,0:T(8,128)(2,1)}), bf16[16,2,32,2048]{3,2,1,0:T(8,128)(2,1)}, u32[]{:S(2)}, u32[]{:S(2)}) async-start(bf16[16,2,32,2048]{3,2,1,0:T(8,128)(2,1)} %stack.4), calls=%async_computation | async-start | bytes 8388608 | tf_op jit(solution)/shard_map/all_to_all | solution.py:20
  74.0 0.0 reduce-scatter.3.cloned.1.call-start
  74.1 0.0 copy-done.3
  74.1 1.3 copy.10
  75.4 0.0 copy-done.2
  75.4 1.4 copy.9
  76.8 1.8 fusion.24
  78.6 3.5 %fusion.16 = f32[512,512]{0,1:T(8,128)S(1)} fusion(f32[512,512]{1,0:T(8,128)S(1)} %fusion.24, f32[512,512]{1,0:T(8,128)S(1)} %copy-done.3), kind=kOutput, calls=%fused_computation.18 | convolution fusion | flops 1610874880 | bytes 3145728 | tf_op jit(solution)/shard_map/dot_general | solution.py:8
  82.1 2.3 %copy.12 = bf16[2,16,32,2048]{3,2,1,0:T(8,128)(2,1)} copy(bf16[2,16,32,2048]{3,2,0,1:T(8,128)(2,1)S(1)} %bitcast.23) | data formatting | bytes 8388608 | tf_op jit(solution)/shard_map/reshape | solution.py:19
  84.4 43.9 %all-to-all-done = bf16[16,2,32,2048]{3,2,1,0:T(8,128)(2,1)} async-done(((bf16[16,2,32,2048]{3,2,1,0:T(8,128)(2,1)}), bf16[16,2,32,2048]{3,2,1,0:T(8,128)(2,1)}, u32[]{:S(2)}, u32[]{:S(2)}) %all-to-all-start) | async-done | bytes 4194336 | tf_op jit(solution)/shard_map/all_to_all | solution.py:20
  128.3 2.7 %copy.11 = bf16[2,16,32,2048]{3,2,1,0:T(8,128)(2,1)S(1)} copy(bf16[2,16,32,2048]{3,2,0,1:T(8,128)(2,1)} %bitcast.1) | data formatting | bytes 8388608 | tf_op jit(solution)/shard_map/reshape | solution.py:19
  130.9 0.8 copy-done.4
  131.7 6.5 %fusion = f32[2,512,1024]{2,1,0:T(8,128)S(1)} fusion(bf16[2,512,2048]{2,1,0:T(8,128)(2,1)S(1)} %bitcast.24, bf16[4096,1024]{1,0:T(8,128)(2,1)} %param.8), kind=kOutput, calls=%fused_computation.2 | convolution fusion | flops 4294967296 | bytes 12582912 | tf_op jit(solution)/shard_map/kra,ac->krc/dot_general | solution.py:30
  138.3 0.0 copy-start.7
  138.3 4.5 %add_negate_fusion = f32[2,512,1024]{2,1,0:T(8,128)S(1)} fusion(f32[2,512,1024]{2,1,0:T(8,128)S(1)} %fusion, bf16[2,512,2048]{2,1,0:T(8,128)(2,1)S(1)} %bitcast.25, bf16[4096,1024]{1,0:T(8,128)(2,1)S(1)} %bitcast.31), kind=kOutput, calls=%fused_computation.6 | convolution fusion | flops 4297064448 | bytes 16777216 | tf_op jit(solution)/shard_map/kra,ac->krc/dot_general | solution.py:30
  142.9 0.1 add_dynamic-update-slice_fusion
  143.0 0.0 copy-start.8
  143.0 0.0 copy-done.5
  143.0 0.0 copy-done.6
  143.0 4.9 %fusion.7 = f32[1024,512]{1,0:T(8,128)} fusion(f32[512,512]{0,1:T(8,128)S(1)} %copy-done.6, f32[512,512]{0,1:T(8,128)S(1)} %copy-done.5, f32[512,512]{0,1:T(8,128)S(1)} %fusion.16, f32[1024,1024]{1,0:T(8,128)S(1)} %bitcast.28), kind=kOutput, calls=%fused_computation.10 | convolution fusion | flops 3225419776 | bytes 7340032 | tf_op jit(solution)/shard_map/dot_general | solution.py:8
  147.9 0.0 reduce-scatter.3.cloned.1.call-update
  148.0 0.0 reduce-scatter.5.cloned.1.call-start
  148.0 6.7 %fusion.6 = f32[1024,512]{1,0:T(8,128)} fusion(f32[512,512]{0,1:T(8,128)} %copy.9, f32[512,512]{0,1:T(8,128)S(1)} %copy-done.5, f32[512,512]{0,1:T(8,128)S(1)} %fusion.16, f32[1024,1024]{1,0:T(8,128)} %bitcast.29), kind=kOutput, calls=%fused_computation.9 | convolution fusion | flops 3225419776 | bytes 7340032 | tf_op jit(solution)/shard_map/dot_general | solution.py:8
  154.8 0.0 reduce-scatter.5.cloned.1.call-update
  154.8 25.3 %reduce-scatter.3.cloned.1.call-done = f32[2,64,512]{2,1,0:T(8,128)} async-done(((f32[2,512,512]{2,1,0:T(8,128)}), f32[2,64,512]{2,1,0:T(8,128)}) %reduce-scatter.3.cloned.1.call-update) | async-done | bytes 262160 | tf_op jit(solution)/shard_map/reduce_scatter | solution.py:55
  180.0 34.9 %reduce-scatter.5.cloned.1.call-done = f32[2,64,512]{2,1,0:T(8,128)} async-done(((f32[2,512,512]{2,1,0:T(8,128)}), f32[2,64,512]{2,1,0:T(8,128)}) %reduce-scatter.5.cloned.1.call-update) | async-done | bytes 262160 | tf_op jit(solution)/shard_map/reduce_scatter | solution.py:55
  214.9 1.9 pad_maximum_fusion
  (15 shorter events, 0.0 us)
Async XLA Ops:
  6.5 70.2 %copy-start = (f32[512,512]{1,0:T(8,128)S(1)}, f32[512,512]{1,0:T(8,128)}, u32[]{:S(2)}) copy-start(f32[512,512]{1,0:T(8,128)} %param.9) | copy-start | bytes 3145732
  69.3 4.7 %copy-start.3 = (f32[512,512]{1,0:T(8,128)S(1)}, f32[512,512]{1,0:T(8,128)}, u32[]{:S(2)}) copy-start(f32[512,512]{1,0:T(8,128)} %param.11) | copy-start | bytes 3145732
  69.3 6.0 %copy-start.2 = (f32[512,512]{1,0:T(8,128)S(1)}, f32[512,512]{1,0:T(8,128)}, u32[]{:S(2)}) copy-start(f32[512,512]{1,0:T(8,128)} %param.10) | copy-start | bytes 3145732
  69.3 59.0 %all-to-all-start = ((bf16[16,2,32,2048]{3,2,1,0:T(8,128)(2,1)}), bf16[16,2,32,2048]{3,2,1,0:T(8,128)(2,1)}, u32[]{:S(2)}, u32[]{:S(2)}) async-start(bf16[16,2,32,2048]{3,2,1,0:T(8,128)(2,1)} %stack.4), calls=%async_computation | async-start | bytes 8388608 | tf_op jit(solution)/shard_map/all_to_all | solution.py:20
  74.0 106.0 %reduce-scatter.3.cloned.1.call-start = ((), (), s32[]{:S(2)}) async-start(), calls=%async_computation.4 | async-start | bytes 2359296 | tf_op jit(solution)/shard_map/reduce_scatter | solution.py:55
  76.7 5.3 %copy-start.1 = (bf16[16,2,32,2048]{3,2,1,0:T(8,128)(2,1)S(1)}, bf16[16,2,32,2048]{3,2,1,0:T(8,128)(2,1)}, u32[]{:S(2)}) copy-start(bf16[16,2,32,2048]{3,2,1,0:T(8,128)(2,1)} %all_to_all.10) | copy-start | bytes 12582916
  128.3 3.4 %copy-start.4 = (bf16[2,16,32,2048]{3,2,1,0:T(8,128)(2,1)S(1)}, bf16[2,16,32,2048]{3,2,1,0:T(8,128)(2,1)}, u32[]{:S(2)}) copy-start(bf16[2,16,32,2048]{3,2,1,0:T(8,128)(2,1)} %copy.12) | copy-start | bytes 12582916
  128.3 10.0 %slice-start = ((s8[8388608]{0:T(1024)(128)(4,1)}), s8[4194304]{0:T(1024)(128)(4,1)S(1)}, s32[]{:S(2)}) async-start(s8[8388608]{0:T(1024)(128)(4,1)} %bitcast.30), calls=%async_computation.6 | async-start | bytes 8388608
  131.7 6.6 %slice-start.1 = ((s8[8388608]{0:T(1024)(128)(4,1)}), s8[4194304]{0:T(1024)(128)(4,1)S(1)}, s32[]{:S(2)}) async-start(s8[8388608]{0:T(1024)(128)(4,1)} %bitcast.30), calls=%async_computation.7 | async-start | bytes 8388608
  138.3 4.6 %copy-start.7 = (f32[2,64,1024]{2,1,0:T(8,128)S(1)}, f32[2,64,1024]{2,1,0:T(8,128)}, u32[]{:S(2)}) copy-start(f32[2,64,1024]{2,1,0:T(8,128)} %param.6) | copy-start | bytes 1572868
  138.3 4.7 %copy-start.5 = (f32[512,512]{0,1:T(8,128)S(1)}, f32[512,512]{0,1:T(8,128)}, u32[]{:S(2)}) copy-start(f32[512,512]{0,1:T(8,128)} %copy.10) | copy-start | bytes 3145732
  138.3 4.7 %copy-start.6 = (f32[512,512]{0,1:T(8,128)S(1)}, f32[512,512]{0,1:T(8,128)}, u32[]{:S(2)}) copy-start(f32[512,512]{0,1:T(8,128)} %copy.9) | copy-start | bytes 3145732
  143.0 5.0 %copy-start.8 = (f32[2,512,1024]{2,1,0:T(8,128)}, f32[2,512,1024]{2,1,0:T(8,128)S(1)}, u32[]{:S(2)}) copy-start(f32[2,512,1024]{2,1,0:T(8,128)S(1)} %add_dynamic-update-slice_fusion) | copy-start | bytes 12582916
  148.0 67.0 %reduce-scatter.5.cloned.1.call-start = ((), (), s32[]{:S(2)}) async-start(), calls=%async_computation.5 | async-start | bytes 2359296 | tf_op jit(solution)/shard_map/reduce_scatter | solution.py:55
Sparse Core Ops, SparseCore 0:
  148.1 31.8 reduce-scatter.2
  182.4 32.4 reduce-scatter.4
